TPU v7x, 32 devices: a whole 2x2x4 slice. The times are simulated.
32 devices in a mesh: band: 8 (over z, y), pair: 4 (over x, core).
Axes of the slice: x: 2, y: 2, z: 4, core: 2. Of those that a mesh axis runs over, the one named last changes fastest.
Arguments:
- orbitals: bfloat16 [32, 262144], P(('band', 'pair')), may hold values from -64 to 64
- partners: int32 [32, 3], P(('band', 'pair')), may hold values from -1 to 31, as said below
Outputs:
- gradient: float32 [32, 262144], P(None, ('band', 'pair'))
Inputs may be any that keep to these rules, and one draw needn't show every extreme that they name: `partners`: slot k of orbital i holds either -1 or i XOR (4 * 2**k); j is listed by i exactly when i is listed by j.
All inputs are finite; a program needn't handle non-finite values.
Results may differ from a plain program's by a relative error of at most 0.0008.
The roundings to bfloat16 on the way count: a program that leaves them out, or rounds other values in their place, can miss the bound.
Values may be sent and summed in bfloat16 or wider, within the bound.
A program may use at most 64 MiB of HBM per device.

v0:
```python
import math
import jax
import jax.numpy as jnp
from jax import lax
from jax.sharding import PartitionSpec as P

NG = 64
PARTNERS = 3
NG3 = 262144
screening = 0.05


def partner(value, axis, distance):
    mask = 2**distance
    pairs = [(source, source ^ mask) for source in range(lax.axis_size(axis))]
    return lax.ppermute(value, axis, pairs)


def sine_table(size):
    index = jnp.arange(size, dtype=jnp.int32) + 1
    product = index[:, None] * index[None, :] % (2 * (size + 1))
    angle = math.pi * product.astype(jnp.float32) / (size + 1)
    return jnp.sqrt(jnp.float32(2.0 / (size + 1))) * jnp.sin(angle)


def eigen_sum(size):
    steps = jnp.arange(size, dtype=jnp.float32) + 1.0
    lam = 2.0 - 2.0 * jnp.cos(math.pi * steps / (size + 1))
    total = lam[:, None, None] + lam[None, :, None] + lam[None, None, :] + screening
    return total.reshape(size, size * size)


def sine_transform(field, table, doubled):
    size = table.shape[0]
    highest = lax.Precision.HIGHEST
    field = jnp.dot(table, field, precision=highest)
    field = jnp.dot(field.reshape(-1, 2 * size), doubled, precision=highest)
    field = jnp.einsum("ky,xyz->xkz", table, field.reshape(size, size, size), precision=highest)
    return field.reshape(size, size * size)


def on_device(orbitals, partners):
    table = sine_table(NG)
    doubled = jnp.kron(jnp.eye(2, dtype=jnp.float32), table)
    denom = eigen_sum(NG)

    def solved(density):
        return sine_transform(sine_transform(density, table, doubled) / denom, table, doubled)

    def nothing(density):
        return jnp.zeros_like(density)

    own = orbitals.reshape(NG, NG * NG).astype(jnp.float32)
    live = partners[0] >= 0
    total = jnp.zeros((NG, NG * NG), jnp.float32)
    for slot in range(PARTNERS):
        arrived = partner(orbitals, "band", slot)
        other = arrived.reshape(NG, NG * NG).astype(jnp.float32)
        density = own * other
        potential = lax.cond(live[slot], solved, nothing, density)
        term = lax.optimization_barrier((potential * other).astype(jnp.bfloat16))
        total = total + jnp.where(live[slot], term.astype(jnp.float32), 0.0)
    applied = total.astype(jnp.bfloat16)
    band_count = lax.axis_size("band")
    pair_count = lax.axis_size("pair")
    cells = NG3 // (band_count * pair_count)
    layout = (1, 1, band_count, pair_count, cells)
    first = orbitals.reshape(layout)
    second = applied.reshape(layout)
    phi_slab, applied_slab = (
        lax.all_to_all(
            lax.all_to_all(first, "band", split_axis=2, concat_axis=0, tiled=True),
            "pair",
            split_axis=3,
            concat_axis=1,
            tiled=True,
        ),
        lax.all_to_all(
            lax.all_to_all(second, "band", split_axis=2, concat_axis=0, tiled=True),
            "pair",
            split_axis=3,
            concat_axis=1,
            tiled=True,
        ),
    )
    count = band_count * pair_count
    phi_slab = phi_slab.reshape(count, cells)
    applied_slab = applied_slab.reshape(count, cells)
    partial_intersection = lax.dot_general(
        phi_slab, applied_slab, (((1,), (1,)), ((), ())), preferred_element_type=jnp.float32
    )
    intersection = lax.psum(partial_intersection * (1.0 / NG3), ("band", "pair"))
    removed = lax.dot_general(
        intersection,
        phi_slab.astype(jnp.float32),
        (((0,), (0,)), ((), ())),
        precision=lax.Precision.HIGHEST,
    )
    return applied_slab.astype(jnp.float32) - removed


def solution(mesh):
    placed = (P(("band", "pair"), None), P(("band", "pair"), None))
    return jax.shard_map(
        on_device, mesh=mesh, in_specs=placed, out_specs=P(None, ("band", "pair")), check_vma=False
    )
```

profile of v0, /device:TPU:0, one launch (start us, length us, event | category | flops | bytes accessed | tf_op | source)
XLA Modules:
  0.0 283.4 jit_solution(6487296302066174337)
XLA Ops:
  0.0 3.1 %collective-permute-start.1 = (bf16[1,262144]{1,0:T(2,128)(2,1)}, bf16[1,262144]{1,0:T(2,128)(2,1)}, u32[]{:S(2)}, u32[]{:S(2)}) collective-permute-start(bf16[1,262144]{1,0:T(2,128)(2,1)} %param.8), channel_id=1, source_target_pairs={{0,8},{4,12},{8,0},{12,4},{16,24},{20,28},{24,16},{28,20},{1,9},{5... | collective-permute-start | bytes 1572872 | tf_op jit(solution)/shard_map/ppermute | solution.py:16
  7.2 11.9 %reduce.4 = bf16[262144]{0:T(1024)(128)(2,1)S(1)} reduce(bf16[1,262144]{1,0:T(2,128)(2,1)} %param.8, bf16[]{:T(256)} %constant.51), dimensions={0}, to_apply=%param.8.reduce_sub_computation | reduce | bytes 1048578 | tf_op args[0]
  20.0 4.5 %all-to-all-start.2 = ((bf16[1,1,8,4,8192]{4,3,1,0,2:T(4,128)(2,1)}), bf16[1,1,8,4,8192]{4,3,1,0,2:T(4,128)(2,1)}, u32[]{:S(2)}, u32[]{:S(2)}) async-start(bf16[1,1,8,4,8192]{4,3,1,0,2:T(4,128)(2,1)} %reshape.218), calls=%async_computation.2 | async-start | bytes 1048576 | tf_op jit(solution)/shard_map/all_to_all | solution.py:72
  24.6 9.7 %convert_reduce_fusion.3 = f32[262144]{0:T(1024)} fusion(bf16[1,262144]{1,0:T(2,128)(2,1)S(1)} %copy-done.1), kind=kLoop, calls=%fused_computation.30 | loop fusion | flops 262144 | bytes 1572864 | tf_op jit(solution)/shard_map/convert_element_type | solution.py:53
  42.3 6.1 %collective-permute-done.1 = bf16[1,262144]{1,0:T(2,128)(2,1)} collective-permute-done((bf16[1,262144]{1,0:T(2,128)(2,1)}, bf16[1,262144]{1,0:T(2,128)(2,1)}, u32[]{:S(2)}, u32[]{:S(2)}) %collective-permute-start.1) | collective-permute-done | bytes 524320 | tf_op jit(solution)/shard_map/ppermute | solution.py:16
  48.4 9.7 %convert_reduce_fusion.1 = f32[262144]{0:T(1024)S(1)} fusion(bf16[1,262144]{1,0:T(2,128)(2,1)} %collective-permute-done.1), kind=kLoop, calls=%fused_computation.28 | loop fusion | flops 262144 | bytes 1572864 | tf_op jit(solution)/shard_map/convert_element_type | solution.py:58
  58.4 39.6 %conditional.4 = (f32[64,4096]{1,0:T(8,128)S(1)}) conditional(s32[]{:T(128)} %convert_element_type.125, () %tuple.25, (f32[64,4096]{1,0:T(8,128)S(1)}, f32[64,4096]{1,0:T(8,128)S(1)}, f32[64,64]{1,0:T(8,128)S(1)}, f32[128,128]{1,0:T(8,128)S(1)}, f32[64,64]{1,0:T(8,128)S(1)}, /*index=5*/f32[64,4096]{1,0:T(8,128)}, f32[64,64]{1,0:T(8,128)S(1)}, ...), branch_computations={%region_2.3_spmd, %region_3.4_spmd} | conditional | flops 1611137024 | bytes 31653896 | solution.py:60
  65.1 6.4 %convolution_bitcast_fusion.7 = f32[64,64,64]{1,2,0:T(8,128)} fusion(f32[64,64,64]{2,1,0:T(8,128)} %reshape.201, f32[64,64]{1,0:T(8,128)S(1)} %get-tuple-element.76), kind=kOutput, calls=%fused_computation.11 | convolution fusion | flops 201326592 | bytes 2113536 | tf_op jit(solution)/shard_map/cond/branch_1_fun/ky,xyz->xkz/dot_general | solution.py:38
  71.4 3.1 %copy.41 = f32[64,64,64]{2,1,0:T(8,128)} copy(f32[64,64,64]{1,2,0:T(8,128)} %convolution_bitcast_fusion.7) | data formatting | bytes 2097152 | tf_op jit(solution)/shard_map/cond/branch_1_fun/ky,xyz->xkz/transpose | solution.py:38
  76.6 3.4 %convolution_bitcast_fusion.4 = f32[64,4096]{1,0:T(8,128)} fusion(f32[64,64]{1,0:T(8,128)S(1)} %get-tuple-element.76, f32[64,4096]{1,0:T(8,128)S(1)} %reshape.202, f32[64,4096]{1,0:T(8,128)} %get-tuple-element.73), kind=kOutput, calls=%fused_computation.8 | convolution fusion | flops 201588736 | bytes 3162112 | tf_op jit(solution)/shard_map/cond/branch_1_fun/dot_general | solution.py:36
  86.3 6.4 %convolution_bitcast_fusion.6 = f32[64,64,64]{1,2,0:T(8,128)} fusion(f32[64,64,64]{2,1,0:T(8,128)} %reshape.204, f32[64,64]{1,0:T(8,128)S(1)} %get-tuple-element.76), kind=kOutput, calls=%fused_computation.10 | convolution fusion | flops 201326592 | bytes 2113536 | tf_op jit(solution)/shard_map/cond/branch_1_fun/ky,xyz->xkz/dot_general | solution.py:38
  92.7 2.9 %copy.43 = f32[64,64,64]{2,1,0:T(8,128)} copy(f32[64,64,64]{1,2,0:T(8,128)} %convolution_bitcast_fusion.6) | data formatting | bytes 2097152 | tf_op jit(solution)/shard_map/cond/branch_1_fun/ky,xyz->xkz/transpose | solution.py:38
  98.8 9.7 %convert_reduce_fusion.2 = f32[262144]{0:T(1024)S(1)} fusion(bf16[1,262144]{1,0:T(2,128)(2,1)} %collective-permute-done), kind=kLoop, calls=%fused_computation.29 | loop fusion | flops 262144 | bytes 1572864 | tf_op jit(solution)/shard_map/convert_element_type | solution.py:58
  108.8 39.2 %conditional.3 = (f32[64,4096]{1,0:T(8,128)S(1)}) conditional(s32[]{:T(128)} %convert_element_type.116, () %tuple.23, (f32[64,4096]{1,0:T(8,128)S(1)}, f32[64,4096]{1,0:T(8,128)S(1)}, f32[64,64]{1,0:T(8,128)S(1)}, f32[128,128]{1,0:T(8,128)S(1)}, f32[64,64]{1,0:T(8,128)S(1)}, /*index=5*/f32[64,4096]{1,0:T(8,128)}, f32[64,64]{1,0:T(8,128)S(1)}, ...), branch_computations={%region_0.1_spmd, %region_1.2_spmd} | conditional | flops 1611137024 | bytes 31653896 | solution.py:60
  114.9 6.4 %convolution_bitcast_fusion.3 = f32[64,64,64]{1,2,0:T(8,128)} fusion(f32[64,64,64]{2,1,0:T(8,128)} %reshape.195, f32[64,64]{1,0:T(8,128)S(1)} %get-tuple-element.55), kind=kOutput, calls=%fused_computation.3 | convolution fusion | flops 201326592 | bytes 2113536 | tf_op jit(solution)/shard_map/cond/branch_1_fun/ky,xyz->xkz/dot_general | solution.py:38
  121.3 3.3 %copy.37 = f32[64,64,64]{2,1,0:T(8,128)} copy(f32[64,64,64]{1,2,0:T(8,128)} %convolution_bitcast_fusion.3) | data formatting | bytes 2097152 | tf_op jit(solution)/shard_map/cond/branch_1_fun/ky,xyz->xkz/transpose | solution.py:38
  126.7 3.4 %convolution_bitcast_fusion = f32[64,4096]{1,0:T(8,128)} fusion(f32[64,64]{1,0:T(8,128)S(1)} %get-tuple-element.55, f32[64,4096]{1,0:T(8,128)S(1)} %reshape.196, f32[64,4096]{1,0:T(8,128)} %get-tuple-element.52), kind=kOutput, calls=%fused_computation | convolution fusion | flops 201588736 | bytes 3162112 | tf_op jit(solution)/shard_map/cond/branch_1_fun/dot_general | solution.py:36
  136.4 6.4 %convolution_bitcast_fusion.2 = f32[64,64,64]{1,2,0:T(8,128)} fusion(f32[64,64,64]{2,1,0:T(8,128)} %reshape.198, f32[64,64]{1,0:T(8,128)S(1)} %get-tuple-element.55), kind=kOutput, calls=%fused_computation.2 | convolution fusion | flops 201326592 | bytes 2113536 | tf_op jit(solution)/shard_map/cond/branch_1_fun/ky,xyz->xkz/dot_general | solution.py:38
  142.7 2.9 %copy.39 = f32[64,64,64]{2,1,0:T(8,128)} copy(f32[64,64,64]{1,2,0:T(8,128)} %convolution_bitcast_fusion.2) | data formatting | bytes 2097152 | tf_op jit(solution)/shard_map/cond/branch_1_fun/ky,xyz->xkz/transpose | solution.py:38
  148.9 9.7 %convert_reduce_fusion = f32[262144]{0:T(1024)S(1)} fusion(bf16[1,262144]{1,0:T(2,128)(2,1)} %collective-permute-done.2), kind=kLoop, calls=%fused_computation.27 | loop fusion | flops 262144 | bytes 1572864 | tf_op jit(solution)/shard_map/convert_element_type | solution.py:58
  158.8 35.7 %conditional.5 = (f32[64,4096]{1,0:T(8,128)S(1)}) conditional(s32[]{:T(128)} %convert_element_type.130, () %tuple.27, (f32[64,4096]{1,0:T(8,128)S(1)}, f32[64,4096]{1,0:T(8,128)S(1)}, f32[64,64]{1,0:T(8,128)S(1)}, f32[128,128]{1,0:T(8,128)S(1)}, f32[64,64]{1,0:T(8,128)S(1)}, /*index=5*/f32[64,4096]{1,0:T(8,128)}, f32[64,64]{1,0:T(8,128)S(1)}, ...), branch_computations={%region_4.5_spmd, %region_5.6_spmd} | conditional | flops 1611137024 | bytes 35848228 | solution.py:60
  164.9 6.4 %convolution_bitcast_fusion.11 = f32[64,64,64]{1,2,0:T(8,128)} fusion(f32[64,64,64]{2,1,0:T(8,128)} %reshape.207, f32[64,64]{1,0:T(8,128)S(1)} %get-tuple-element.85), kind=kOutput, calls=%fused_computation.19 | convolution fusion | flops 201326592 | bytes 2113536 | tf_op jit(solution)/shard_map/cond/branch_1_fun/ky,xyz->xkz/dot_general | solution.py:38
  171.3 3.1 %copy.45 = f32[64,64,64]{2,1,0:T(8,128)} copy(f32[64,64,64]{1,2,0:T(8,128)} %convolution_bitcast_fusion.11) | data formatting | bytes 2097152 | tf_op jit(solution)/shard_map/cond/branch_1_fun/ky,xyz->xkz/transpose | solution.py:38
  182.8 6.4 %convolution_bitcast_fusion.10 = f32[64,64,64]{1,2,0:T(8,128)} fusion(f32[64,64,64]{2,1,0:T(8,128)} %reshape.210, f32[64,64]{1,0:T(8,128)S(1)} %get-tuple-element.85), kind=kOutput, calls=%fused_computation.18 | convolution fusion | flops 201326592 | bytes 2113536 | tf_op jit(solution)/shard_map/cond/branch_1_fun/ky,xyz->xkz/dot_general | solution.py:38
  189.2 2.9 %copy.47 = f32[64,64,64]{2,1,0:T(8,128)} copy(f32[64,64,64]{1,2,0:T(8,128)} %convolution_bitcast_fusion.10) | data formatting | bytes 2097152 | tf_op jit(solution)/shard_map/cond/branch_1_fun/ky,xyz->xkz/transpose | solution.py:38
  199.0 6.2 %all-to-all-start = ((bf16[1,1,8,4,8192]{4,3,1,0,2:T(4,128)(2,1)}), bf16[1,1,8,4,8192]{4,3,1,0,2:T(4,128)(2,1)S(1)}, u32[]{:S(2)}, u32[]{:S(2)}) async-start(bf16[1,1,8,4,8192]{4,3,1,0,2:T(4,128)(2,1)} %reshape.216), calls=%async_computation | async-start | bytes 1048576 | tf_op jit(solution)/shard_map/all_to_all | solution.py:79
  207.4 10.4 %all-to-all-done = bf16[1,1,8,4,8192]{4,3,1,0,2:T(4,128)(2,1)S(1)} async-done(((bf16[1,1,8,4,8192]{4,3,1,0,2:T(4,128)(2,1)}), bf16[1,1,8,4,8192]{4,3,1,0,2:T(4,128)(2,1)S(1)}, u32[]{:S(2)}, u32[]{:S(2)}) %all-to-all-start) | async-done | bytes 524320 | tf_op jit(solution)/shard_map/all_to_all | solution.py:79
  217.8 3.5 %all-to-all-start.3 = ((bf16[8,1,1,4,8192]{4,0,2,1,3:T(8,128)(2,1)}), bf16[8,1,1,4,8192]{4,0,2,1,3:T(8,128)(2,1)S(1)}, u32[]{:S(2)}, u32[]{:S(2)}) async-start(bf16[8,1,1,4,8192]{4,0,2,1,3:T(8,128)(2,1)} %copy.50), calls=%async_computation.3 | async-start | bytes 1048576 | tf_op jit(solution)/shard_map/all_to_all | solution.py:71
  222.4 7.7 %all-to-all-done.3 = bf16[8,1,1,4,8192]{4,0,2,1,3:T(8,128)(2,1)S(1)} async-done(((bf16[8,1,1,4,8192]{4,0,2,1,3:T(8,128)(2,1)}), bf16[8,1,1,4,8192]{4,0,2,1,3:T(8,128)(2,1)S(1)}, u32[]{:S(2)}, u32[]{:S(2)}) %all-to-all-start.3) | async-done | bytes 524320 | tf_op jit(solution)/shard_map/all_to_all | solution.py:71
  230.1 3.5 %all-to-all-start.1 = ((bf16[8,1,1,4,8192]{4,0,2,1,3:T(8,128)(2,1)}), bf16[8,1,1,4,8192]{4,0,2,1,3:T(8,128)(2,1)S(1)}, u32[]{:S(2)}, u32[]{:S(2)}) async-start(bf16[8,1,1,4,8192]{4,0,2,1,3:T(8,128)(2,1)} %copy.48), calls=%async_computation.1 | async-start | bytes 1048576 | tf_op jit(solution)/shard_map/all_to_all | solution.py:78
  234.1 8.2 %all-to-all-done.1 = bf16[8,1,1,4,8192]{4,0,2,1,3:T(8,128)(2,1)S(1)} async-done(((bf16[8,1,1,4,8192]{4,0,2,1,3:T(8,128)(2,1)}), bf16[8,1,1,4,8192]{4,0,2,1,3:T(8,128)(2,1)S(1)}, u32[]{:S(2)}, u32[]{:S(2)}) %all-to-all-start.1) | async-done | bytes 524320 | tf_op jit(solution)/shard_map/all_to_all | solution.py:78
  243.2 38.5 %psum.7 = f32[32,32]{0,1:T(8,128)S(1)} all-reduce(f32[32,32]{0,1:T(8,128)S(1)} %fusion.12), channel_id=1, replica_groups=mesh['band'=8,'pair'=4] {'band','pair'}, use_global_device_ids=true, to_apply=%region_6.7 | all-reduce | flops 1024 | bytes 8192 | tf_op jit(solution)/shard_map/psum | solution.py:92
  (77 shorter events, 74.0 us)
Async XLA Ops:
  0.0 24.6 %copy-start.1 = (bf16[1,262144]{1,0:T(2,128)(2,1)S(1)}, bf16[1,262144]{1,0:T(2,128)(2,1)}, u32[]{:S(2)}) copy-start(bf16[1,262144]{1,0:T(2,128)(2,1)} %param.8) | copy-start | bytes 1572868
  0.0 48.4 %collective-permute-start.1 = (bf16[1,262144]{1,0:T(2,128)(2,1)}, bf16[1,262144]{1,0:T(2,128)(2,1)}, u32[]{:S(2)}, u32[]{:S(2)}) collective-permute-start(bf16[1,262144]{1,0:T(2,128)(2,1)} %param.8), channel_id=1, source_target_pairs={{0,8},{4,12},{8,0},{12,4},{16,24},{20,28},{24,16},{28,20},{1,9},{5... | collective-permute-start | bytes 1572872 | tf_op jit(solution)/shard_map/ppermute | solution.py:16
  3.1 95.8 %collective-permute-start = (bf16[1,262144]{1,0:T(2,128)(2,1)}, bf16[1,262144]{1,0:T(2,128)(2,1)}, u32[]{:S(2)}, u32[]{:S(2)}) collective-permute-start(bf16[1,262144]{1,0:T(2,128)(2,1)} %param.8), channel_id=1, source_target_pairs={{0,4},{4,0},{8,12},{12,8},{16,20},{20,16},{24,28},{28,24},{1,5},{5... | collective-permute-start | bytes 1572872 | tf_op jit(solution)/shard_map/ppermute | solution.py:16
  4.6 144.3 %collective-permute-start.2 = (bf16[1,262144]{1,0:T(2,128)(2,1)}, bf16[1,262144]{1,0:T(2,128)(2,1)}, u32[]{:S(2)}, u32[]{:S(2)}) collective-permute-start(bf16[1,262144]{1,0:T(2,128)(2,1)} %param.8), channel_id=1, source_target_pairs={{0,16},{4,20},{8,24},{12,28},{16,0},{20,4},{24,8},{28,12},{1,17},{... | collective-permute-start | bytes 1572872 | tf_op jit(solution)/shard_map/ppermute | solution.py:16
  20.0 179.0 %all-to-all-start.2 = ((bf16[1,1,8,4,8192]{4,3,1,0,2:T(4,128)(2,1)}), bf16[1,1,8,4,8192]{4,3,1,0,2:T(4,128)(2,1)}, u32[]{:S(2)}, u32[]{:S(2)}) async-start(bf16[1,1,8,4,8192]{4,3,1,0,2:T(4,128)(2,1)} %reshape.218), calls=%async_computation.2 | async-start | bytes 1048576 | tf_op jit(solution)/shard_map/all_to_all | solution.py:72
  35.4 3.3 %copy-start.5 = (s32[1,3]{1,0:T(1,128)S(1)}, s32[1,3]{1,0:T(1,128)}, u32[]{:S(2)}) copy-start(s32[1,3]{1,0:T(1,128)} %param.9) | copy-start | bytes 40
  37.1 4.1 %copy-start = (f32[64,4096]{1,0:T(8,128)S(1)}, f32[64,4096]{1,0:T(8,128)}, u32[]{:S(2)}) copy-start(f32[64,4096]{1,0:T(8,128)} %add.210) | copy-start | bytes 3145732
  174.4 2.2 copy-start.4
  194.5 1.0 copy-start.2
  194.5 1.2 copy-start.3
  199.0 18.8 %all-to-all-start = ((bf16[1,1,8,4,8192]{4,3,1,0,2:T(4,128)(2,1)}), bf16[1,1,8,4,8192]{4,3,1,0,2:T(4,128)(2,1)S(1)}, u32[]{:S(2)}, u32[]{:S(2)}) async-start(bf16[1,1,8,4,8192]{4,3,1,0,2:T(4,128)(2,1)} %reshape.216), calls=%async_computation | async-start | bytes 1048576 | tf_op jit(solution)/shard_map/all_to_all | solution.py:79
  217.8 12.3 %all-to-all-start.3 = ((bf16[8,1,1,4,8192]{4,0,2,1,3:T(8,128)(2,1)}), bf16[8,1,1,4,8192]{4,0,2,1,3:T(8,128)(2,1)S(1)}, u32[]{:S(2)}, u32[]{:S(2)}) async-start(bf16[8,1,1,4,8192]{4,0,2,1,3:T(8,128)(2,1)} %copy.50), calls=%async_computation.3 | async-start | bytes 1048576 | tf_op jit(solution)/shard_map/all_to_all | solution.py:71
  230.1 12.3 %all-to-all-start.1 = ((bf16[8,1,1,4,8192]{4,0,2,1,3:T(8,128)(2,1)}), bf16[8,1,1,4,8192]{4,0,2,1,3:T(8,128)(2,1)S(1)}, u32[]{:S(2)}, u32[]{:S(2)}) async-start(bf16[8,1,1,4,8192]{4,0,2,1,3:T(8,128)(2,1)} %copy.48), calls=%async_computation.1 | async-start | bytes 1048576 | tf_op jit(solution)/shard_map/all_to_all | solution.py:78
where the time goes:
time: 289 us; the launch traced here: 283 us
  matrix products  64.3 us (22%)
  local copies, waits for them, and re-layouts  63.2 us (22%)
  other arithmetic  56.3 us (19%)
  blocking collectives  38.5 us (13%)
  waiting for transfers between devices  32.5 us (11%)
  starting transfers between devices  24.8 us (9%)
    psum x1, blocking collectives, on_device(): lax.psum(partial_intersection * (1.0 / NG3), ('band', 'pair'))  38.5 us
    dot_general x6, matrix products, sine_transform(): jnp.einsum('ky,xyz->xkz', table, field.reshape(size, size, size), precisi...  38.2 us
    convert_element_type x3, other arithmetic, on_device(): other = arrived.reshape(NG, NG * NG).astype(jnp.float32)  29.2 us
    transpose x6, local copies, waits for them, and re-layouts, sine_transform(): jnp.einsum('ky,xyz->xkz', table, field.reshape(size, size, size), precisi...  18.1 us
    reshape x6, local copies, waits for them, and re-layouts, sine_transform(): return field.reshape(size, size * size)  12.8 us
    dot_general x6, matrix products, sine_transform(): field = jnp.dot(table, field, precision=highest)  12.4 us
    dot_general x6, matrix products, sine_transform(): field = jnp.dot(field.reshape(-1, 2 * size), doubled, precision=highest)  11.9 us
    unnamed x1, other arithmetic  11.9 us
  transfers between devices with their start and end apart: 7, of which 4 were waited for; matrix products, arithmetic and copies ran while one was open for 64% of the time, Pallas kernels for 0%

commit v1 on v0

--- a/solution.py
+++ b/solution.py
@@ -89,7 +89,9 @@
     partial_intersection = lax.dot_general(
         phi_slab, applied_slab, (((1,), (1,)), ((), ())), preferred_element_type=jnp.float32
     )
-    intersection = lax.psum(partial_intersection * (1.0 / NG3), ("band", "pair"))
+    intersection = jnp.sum(
+        lax.all_gather(partial_intersection * (1.0 / NG3), axis_name=("band", "pair")), axis=0
+    )
     removed = lax.dot_general(
         intersection,
         phi_slab.astype(jnp.float32),

time: 289 us -> 291 us (level)
    all_gather x0 -> x1, blocking collectives: none -> 40 us  [on_device(): lax.all_gather(partial_intersection * (1.0 / NG3), axis_name=('band', 'pa...]
    psum x1 -> x0, blocking collectives: 38.5 us -> none  [on_device(): lax.psum(partial_intersection * (1.0 / NG3), ('band', 'pair'))]
    unnamed x1 -> x2, other arithmetic: 11.9 us -> 12 us
  transfers between devices with their start and end apart: 7 -> 7, of which waited for: 4 -> 4; matrix products, arithmetic and copies ran while one was open for 64% -> 63% of each run, Pallas kernels for 0% -> 0%
where the time goes in v1:
time: 291 us; the launch traced here: 285 us
  matrix products  64.4 us (22%)
  local copies, waits for them, and re-layouts  63.3 us (22%)
  other arithmetic  56.4 us (19%)
  blocking collectives  40 us (14%)
  waiting for transfers between devices  32.5 us (11%)
  starting transfers between devices  24.8 us (9%)
    all_gather x1, blocking collectives, on_device(): lax.all_gather(partial_intersection * (1.0 / NG3), axis_name=('band', 'pa...  40 us
    dot_general x6, matrix products, sine_transform(): jnp.einsum('ky,xyz->xkz', table, field.reshape(size, size, size), precisi...  38.2 us
    convert_element_type x3, other arithmetic, on_device(): other = arrived.reshape(NG, NG * NG).astype(jnp.float32)  29.2 us
    transpose x6, local copies, waits for them, and re-layouts, sine_transform(): jnp.einsum('ky,xyz->xkz', table, field.reshape(size, size, size), precisi...  18.1 us
    reshape x6, local copies, waits for them, and re-layouts, sine_transform(): return field.reshape(size, size * size)  12.8 us
    dot_general x6, matrix products, sine_transform(): field = jnp.dot(table, field, precision=highest)  12.4 us
    unnamed x2, other arithmetic  12 us
    dot_general x6, matrix products, sine_transform(): field = jnp.dot(field.reshape(-1, 2 * size), doubled, precision=highest)  11.9 us
  transfers between devices with their start and end apart: 7, of which 4 were waited for; matrix products, arithmetic and copies ran while one was open for 63% of the time, Pallas kernels for 0%

profile of v1, /device:TPU:0, one launch (start us, length us, event | category | flops | bytes accessed | tf_op | source)
XLA Modules:
  0.0 285.2 jit_solution(16599259336757993321)
XLA Ops:
  0.0 3.1 %collective-permute-start.1 = (bf16[1,262144]{1,0:T(2,128)(2,1)}, bf16[1,262144]{1,0:T(2,128)(2,1)}, u32[]{:S(2)}, u32[]{:S(2)}) collective-permute-start(bf16[1,262144]{1,0:T(2,128)(2,1)} %param.8), channel_id=1, source_target_pairs={{0,8},{4,12},{8,0},{12,4},{16,24},{20,28},{24,16},{28,20},{1,9},{5... | collective-permute-start | bytes 1572872 | tf_op jit(solution)/shard_map/ppermute | solution.py:16
  7.2 11.9 %reduce.4 = bf16[262144]{0:T(1024)(128)(2,1)S(1)} reduce(bf16[1,262144]{1,0:T(2,128)(2,1)} %param.8, bf16[]{:T(256)} %constant.51), dimensions={0}, to_apply=%param.8.reduce_sub_computation | reduce | bytes 1048578 | tf_op args[0]
  20.0 4.5 %all-to-all-start.2 = ((bf16[1,1,8,4,8192]{4,3,1,0,2:T(4,128)(2,1)}), bf16[1,1,8,4,8192]{4,3,1,0,2:T(4,128)(2,1)}, u32[]{:S(2)}, u32[]{:S(2)}) async-start(bf16[1,1,8,4,8192]{4,3,1,0,2:T(4,128)(2,1)} %reshape.218), calls=%async_computation.2 | async-start | bytes 1048576 | tf_op jit(solution)/shard_map/all_to_all | solution.py:72
  24.6 9.7 %convert_reduce_fusion.3 = f32[262144]{0:T(1024)} fusion(bf16[1,262144]{1,0:T(2,128)(2,1)S(1)} %copy-done.1), kind=kLoop, calls=%fused_computation.30 | loop fusion | flops 262144 | bytes 1572864 | tf_op jit(solution)/shard_map/convert_element_type | solution.py:53
  42.3 6.1 %collective-permute-done.1 = bf16[1,262144]{1,0:T(2,128)(2,1)} collective-permute-done((bf16[1,262144]{1,0:T(2,128)(2,1)}, bf16[1,262144]{1,0:T(2,128)(2,1)}, u32[]{:S(2)}, u32[]{:S(2)}) %collective-permute-start.1) | collective-permute-done | bytes 524320 | tf_op jit(solution)/shard_map/ppermute | solution.py:16
  48.4 9.7 %convert_reduce_fusion.1 = f32[262144]{0:T(1024)S(1)} fusion(bf16[1,262144]{1,0:T(2,128)(2,1)} %collective-permute-done.1), kind=kLoop, calls=%fused_computation.28 | loop fusion | flops 262144 | bytes 1572864 | tf_op jit(solution)/shard_map/convert_element_type | solution.py:58
  58.4 39.6 %conditional.4 = (f32[64,4096]{1,0:T(8,128)S(1)}) conditional(s32[]{:T(128)} %convert_element_type.125, () %tuple.25, (f32[64,4096]{1,0:T(8,128)S(1)}, f32[64,4096]{1,0:T(8,128)S(1)}, f32[64,64]{1,0:T(8,128)S(1)}, f32[128,128]{1,0:T(8,128)S(1)}, f32[64,64]{1,0:T(8,128)S(1)}, /*index=5*/f32[64,4096]{1,0:T(8,128)}, f32[64,64]{1,0:T(8,128)S(1)}, ...), branch_computations={%region_2.3_spmd, %region_3.4_spmd} | conditional | flops 1611137024 | bytes 31653896 | solution.py:60
  65.1 6.4 %convolution_bitcast_fusion.7 = f32[64,64,64]{1,2,0:T(8,128)} fusion(f32[64,64,64]{2,1,0:T(8,128)} %reshape.201, f32[64,64]{1,0:T(8,128)S(1)} %get-tuple-element.76), kind=kOutput, calls=%fused_computation.11 | convolution fusion | flops 201326592 | bytes 2113536 | tf_op jit(solution)/shard_map/cond/branch_1_fun/ky,xyz->xkz/dot_general | solution.py:38
  71.4 3.1 %copy.43 = f32[64,64,64]{2,1,0:T(8,128)} copy(f32[64,64,64]{1,2,0:T(8,128)} %convolution_bitcast_fusion.7) | data formatting | bytes 2097152 | tf_op jit(solution)/shard_map/cond/branch_1_fun/ky,xyz->xkz/transpose | solution.py:38
  76.6 3.4 %convolution_bitcast_fusion.4 = f32[64,4096]{1,0:T(8,128)} fusion(f32[64,64]{1,0:T(8,128)S(1)} %get-tuple-element.76, f32[64,4096]{1,0:T(8,128)S(1)} %reshape.202, f32[64,4096]{1,0:T(8,128)} %get-tuple-element.73), kind=kOutput, calls=%fused_computation.8 | convolution fusion | flops 201588736 | bytes 3162112 | tf_op jit(solution)/shard_map/cond/branch_1_fun/dot_general | solution.py:36
  86.3 6.4 %convolution_bitcast_fusion.6 = f32[64,64,64]{1,2,0:T(8,128)} fusion(f32[64,64,64]{2,1,0:T(8,128)} %reshape.204, f32[64,64]{1,0:T(8,128)S(1)} %get-tuple-element.76), kind=kOutput, calls=%fused_computation.10 | convolution fusion | flops 201326592 | bytes 2113536 | tf_op jit(solution)/shard_map/cond/branch_1_fun/ky,xyz->xkz/dot_general | solution.py:38
  92.7 2.9 %copy.45 = f32[64,64,64]{2,1,0:T(8,128)} copy(f32[64,64,64]{1,2,0:T(8,128)} %convolution_bitcast_fusion.6) | data formatting | bytes 2097152 | tf_op jit(solution)/shard_map/cond/branch_1_fun/ky,xyz->xkz/transpose | solution.py:38
  98.8 9.7 %convert_reduce_fusion.2 = f32[262144]{0:T(1024)S(1)} fusion(bf16[1,262144]{1,0:T(2,128)(2,1)} %collective-permute-done), kind=kLoop, calls=%fused_computation.29 | loop fusion | flops 262144 | bytes 1572864 | tf_op jit(solution)/shard_map/convert_element_type | solution.py:58
  108.8 39.2 %conditional.3 = (f32[64,4096]{1,0:T(8,128)S(1)}) conditional(s32[]{:T(128)} %convert_element_type.116, () %tuple.23, (f32[64,4096]{1,0:T(8,128)S(1)}, f32[64,4096]{1,0:T(8,128)S(1)}, f32[64,64]{1,0:T(8,128)S(1)}, f32[128,128]{1,0:T(8,128)S(1)}, f32[64,64]{1,0:T(8,128)S(1)}, /*index=5*/f32[64,4096]{1,0:T(8,128)}, f32[64,64]{1,0:T(8,128)S(1)}, ...), branch_computations={%region_0.1_spmd, %region_1.2_spmd} | conditional | flops 1611137024 | bytes 31653896 | solution.py:60
  114.9 6.4 %convolution_bitcast_fusion.3 = f32[64,64,64]{1,2,0:T(8,128)} fusion(f32[64,64,64]{2,1,0:T(8,128)} %reshape.195, f32[64,64]{1,0:T(8,128)S(1)} %get-tuple-element.55), kind=kOutput, calls=%fused_computation.3 | convolution fusion | flops 201326592 | bytes 2113536 | tf_op jit(solution)/shard_map/cond/branch_1_fun/ky,xyz->xkz/dot_general | solution.py:38
  121.3 3.3 %copy.39 = f32[64,64,64]{2,1,0:T(8,128)} copy(f32[64,64,64]{1,2,0:T(8,128)} %convolution_bitcast_fusion.3) | data formatting | bytes 2097152 | tf_op jit(solution)/shard_map/cond/branch_1_fun/ky,xyz->xkz/transpose | solution.py:38
  126.7 3.4 %convolution_bitcast_fusion = f32[64,4096]{1,0:T(8,128)} fusion(f32[64,64]{1,0:T(8,128)S(1)} %get-tuple-element.55, f32[64,4096]{1,0:T(8,128)S(1)} %reshape.196, f32[64,4096]{1,0:T(8,128)} %get-tuple-element.52), kind=kOutput, calls=%fused_computation | convolution fusion | flops 201588736 | bytes 3162112 | tf_op jit(solution)/shard_map/cond/branch_1_fun/dot_general | solution.py:36
  136.4 6.4 %convolution_bitcast_fusion.2 = f32[64,64,64]{1,2,0:T(8,128)} fusion(f32[64,64,64]{2,1,0:T(8,128)} %reshape.198, f32[64,64]{1,0:T(8,128)S(1)} %get-tuple-element.55), kind=kOutput, calls=%fused_computation.2 | convolution fusion | flops 201326592 | bytes 2113536 | tf_op jit(solution)/shard_map/cond/branch_1_fun/ky,xyz->xkz/dot_general | solution.py:38
  142.7 2.9 %copy.41 = f32[64,64,64]{2,1,0:T(8,128)} copy(f32[64,64,64]{1,2,0:T(8,128)} %convolution_bitcast_fusion.2) | data formatting | bytes 2097152 | tf_op jit(solution)/shard_map/cond/branch_1_fun/ky,xyz->xkz/transpose | solution.py:38
  148.9 9.7 %convert_reduce_fusion = f32[262144]{0:T(1024)S(1)} fusion(bf16[1,262144]{1,0:T(2,128)(2,1)} %collective-permute-done.2), kind=kLoop, calls=%fused_computation.27 | loop fusion | flops 262144 | bytes 1572864 | tf_op jit(solution)/shard_map/convert_element_type | solution.py:58
  158.8 35.7 %conditional.5 = (f32[64,4096]{1,0:T(8,128)S(1)}) conditional(s32[]{:T(128)} %convert_element_type.130, () %tuple.27, (f32[64,4096]{1,0:T(8,128)S(1)}, f32[64,4096]{1,0:T(8,128)S(1)}, f32[64,64]{1,0:T(8,128)S(1)}, f32[128,128]{1,0:T(8,128)S(1)}, f32[64,64]{1,0:T(8,128)S(1)}, /*index=5*/f32[64,4096]{1,0:T(8,128)}, f32[64,64]{1,0:T(8,128)S(1)}, ...), branch_computations={%region_4.5_spmd, %region_5.6_spmd} | conditional | flops 1611137024 | bytes 35848228 | solution.py:60
  164.9 6.4 %convolution_bitcast_fusion.11 = f32[64,64,64]{1,2,0:T(8,128)} fusion(f32[64,64,64]{2,1,0:T(8,128)} %reshape.207, f32[64,64]{1,0:T(8,128)S(1)} %get-tuple-element.85), kind=kOutput, calls=%fused_computation.19 | convolution fusion | flops 201326592 | bytes 2113536 | tf_op jit(solution)/shard_map/cond/branch_1_fun/ky,xyz->xkz/dot_general | solution.py:38
  171.3 3.1 %copy.47 = f32[64,64,64]{2,1,0:T(8,128)} copy(f32[64,64,64]{1,2,0:T(8,128)} %convolution_bitcast_fusion.11) | data formatting | bytes 2097152 | tf_op jit(solution)/shard_map/cond/branch_1_fun/ky,xyz->xkz/transpose | solution.py:38
  182.8 6.4 %convolution_bitcast_fusion.10 = f32[64,64,64]{1,2,0:T(8,128)} fusion(f32[64,64,64]{2,1,0:T(8,128)} %reshape.210, f32[64,64]{1,0:T(8,128)S(1)} %get-tuple-element.85), kind=kOutput, calls=%fused_computation.18 | convolution fusion | flops 201326592 | bytes 2113536 | tf_op jit(solution)/shard_map/cond/branch_1_fun/ky,xyz->xkz/dot_general | solution.py:38
  189.2 2.9 %copy.49 = f32[64,64,64]{2,1,0:T(8,128)} copy(f32[64,64,64]{1,2,0:T(8,128)} %convolution_bitcast_fusion.10) | data formatting | bytes 2097152 | tf_op jit(solution)/shard_map/cond/branch_1_fun/ky,xyz->xkz/transpose | solution.py:38
  199.0 6.2 %all-to-all-start = ((bf16[1,1,8,4,8192]{4,3,1,0,2:T(4,128)(2,1)}), bf16[1,1,8,4,8192]{4,3,1,0,2:T(4,128)(2,1)S(1)}, u32[]{:S(2)}, u32[]{:S(2)}) async-start(bf16[1,1,8,4,8192]{4,3,1,0,2:T(4,128)(2,1)} %reshape.216), calls=%async_computation | async-start | bytes 1048576 | tf_op jit(solution)/shard_map/all_to_all | solution.py:79
  207.4 10.4 %all-to-all-done = bf16[1,1,8,4,8192]{4,3,1,0,2:T(4,128)(2,1)S(1)} async-done(((bf16[1,1,8,4,8192]{4,3,1,0,2:T(4,128)(2,1)}), bf16[1,1,8,4,8192]{4,3,1,0,2:T(4,128)(2,1)S(1)}, u32[]{:S(2)}, u32[]{:S(2)}) %all-to-all-start) | async-done | bytes 524320 | tf_op jit(solution)/shard_map/all_to_all | solution.py:79
  217.8 3.5 %all-to-all-start.3 = ((bf16[8,1,1,4,8192]{4,0,2,1,3:T(8,128)(2,1)}), bf16[8,1,1,4,8192]{4,0,2,1,3:T(8,128)(2,1)S(1)}, u32[]{:S(2)}, u32[]{:S(2)}) async-start(bf16[8,1,1,4,8192]{4,0,2,1,3:T(8,128)(2,1)} %copy.52), calls=%async_computation.3 | async-start | bytes 1048576 | tf_op jit(solution)/shard_map/all_to_all | solution.py:71
  222.4 7.7 %all-to-all-done.3 = bf16[8,1,1,4,8192]{4,0,2,1,3:T(8,128)(2,1)S(1)} async-done(((bf16[8,1,1,4,8192]{4,0,2,1,3:T(8,128)(2,1)}), bf16[8,1,1,4,8192]{4,0,2,1,3:T(8,128)(2,1)S(1)}, u32[]{:S(2)}, u32[]{:S(2)}) %all-to-all-start.3) | async-done | bytes 524320 | tf_op jit(solution)/shard_map/all_to_all | solution.py:71
  230.1 3.5 %all-to-all-start.1 = ((bf16[8,1,1,4,8192]{4,0,2,1,3:T(8,128)(2,1)}), bf16[8,1,1,4,8192]{4,0,2,1,3:T(8,128)(2,1)S(1)}, u32[]{:S(2)}, u32[]{:S(2)}) async-start(bf16[8,1,1,4,8192]{4,0,2,1,3:T(8,128)(2,1)} %copy.50), calls=%async_computation.1 | async-start | bytes 1048576 | tf_op jit(solution)/shard_map/all_to_all | solution.py:78
  234.1 8.2 %all-to-all-done.1 = bf16[8,1,1,4,8192]{4,0,2,1,3:T(8,128)(2,1)S(1)} async-done(((bf16[8,1,1,4,8192]{4,0,2,1,3:T(8,128)(2,1)}), bf16[8,1,1,4,8192]{4,0,2,1,3:T(8,128)(2,1)S(1)}, u32[]{:S(2)}, u32[]{:S(2)}) %all-to-all-start.1) | async-done | bytes 524320 | tf_op jit(solution)/shard_map/all_to_all | solution.py:78
  243.2 40.0 %all-gather = f32[1024,32]{1,0:T(8,128)S(1)} all-gather(f32[32,32]{1,0:T(8,128)S(1)} %copy.54), channel_id=2, replica_groups=mesh['band'=8,'pair'=4] {'band','pair'}, dimensions={0}, use_global_device_ids=true | all-gather | bytes 135168 | tf_op jit(solution)/shard_map/all_gather | solution.py:93
  (79 shorter events, 74.2 us)
Async XLA Ops:
  0.0 24.6 %copy-start.1 = (bf16[1,262144]{1,0:T(2,128)(2,1)S(1)}, bf16[1,262144]{1,0:T(2,128)(2,1)}, u32[]{:S(2)}) copy-start(bf16[1,262144]{1,0:T(2,128)(2,1)} %param.8) | copy-start | bytes 1572868
  0.0 48.4 %collective-permute-start.1 = (bf16[1,262144]{1,0:T(2,128)(2,1)}, bf16[1,262144]{1,0:T(2,128)(2,1)}, u32[]{:S(2)}, u32[]{:S(2)}) collective-permute-start(bf16[1,262144]{1,0:T(2,128)(2,1)} %param.8), channel_id=1, source_target_pairs={{0,8},{4,12},{8,0},{12,4},{16,24},{20,28},{24,16},{28,20},{1,9},{5... | collective-permute-start | bytes 1572872 | tf_op jit(solution)/shard_map/ppermute | solution.py:16
  3.1 95.8 %collective-permute-start = (bf16[1,262144]{1,0:T(2,128)(2,1)}, bf16[1,262144]{1,0:T(2,128)(2,1)}, u32[]{:S(2)}, u32[]{:S(2)}) collective-permute-start(bf16[1,262144]{1,0:T(2,128)(2,1)} %param.8), channel_id=1, source_target_pairs={{0,4},{4,0},{8,12},{12,8},{16,20},{20,16},{24,28},{28,24},{1,5},{5... | collective-permute-start | bytes 1572872 | tf_op jit(solution)/shard_map/ppermute | solution.py:16
  4.6 144.3 %collective-permute-start.2 = (bf16[1,262144]{1,0:T(2,128)(2,1)}, bf16[1,262144]{1,0:T(2,128)(2,1)}, u32[]{:S(2)}, u32[]{:S(2)}) collective-permute-start(bf16[1,262144]{1,0:T(2,128)(2,1)} %param.8), channel_id=1, source_target_pairs={{0,16},{4,20},{8,24},{12,28},{16,0},{20,4},{24,8},{28,12},{1,17},{... | collective-permute-start | bytes 1572872 | tf_op jit(solution)/shard_map/ppermute | solution.py:16
  20.0 179.0 %all-to-all-start.2 = ((bf16[1,1,8,4,8192]{4,3,1,0,2:T(4,128)(2,1)}), bf16[1,1,8,4,8192]{4,3,1,0,2:T(4,128)(2,1)}, u32[]{:S(2)}, u32[]{:S(2)}) async-start(bf16[1,1,8,4,8192]{4,3,1,0,2:T(4,128)(2,1)} %reshape.218), calls=%async_computation.2 | async-start | bytes 1048576 | tf_op jit(solution)/shard_map/all_to_all | solution.py:72
  35.4 3.3 %copy-start.5 = (s32[1,3]{1,0:T(1,128)S(1)}, s32[1,3]{1,0:T(1,128)}, u32[]{:S(2)}) copy-start(s32[1,3]{1,0:T(1,128)} %param.9) | copy-start | bytes 40
  37.1 4.1 %copy-start = (f32[64,4096]{1,0:T(8,128)S(1)}, f32[64,4096]{1,0:T(8,128)}, u32[]{:S(2)}) copy-start(f32[64,4096]{1,0:T(8,128)} %add.208) | copy-start | bytes 3145732
  174.4 2.2 copy-start.4
  194.5 1.0 copy-start.2
  194.5 1.2 copy-start.3
  199.0 18.8 %all-to-all-start = ((bf16[1,1,8,4,8192]{4,3,1,0,2:T(4,128)(2,1)}), bf16[1,1,8,4,8192]{4,3,1,0,2:T(4,128)(2,1)S(1)}, u32[]{:S(2)}, u32[]{:S(2)}) async-start(bf16[1,1,8,4,8192]{4,3,1,0,2:T(4,128)(2,1)} %reshape.216), calls=%async_computation | async-start | bytes 1048576 | tf_op jit(solution)/shard_map/all_to_all | solution.py:79
  217.8 12.3 %all-to-all-start.3 = ((bf16[8,1,1,4,8192]{4,0,2,1,3:T(8,128)(2,1)}), bf16[8,1,1,4,8192]{4,0,2,1,3:T(8,128)(2,1)S(1)}, u32[]{:S(2)}, u32[]{:S(2)}) async-start(bf16[8,1,1,4,8192]{4,0,2,1,3:T(8,128)(2,1)} %copy.52), calls=%async_computation.3 | async-start | bytes 1048576 | tf_op jit(solution)/shard_map/all_to_all | solution.py:71
  230.1 12.3 %all-to-all-start.1 = ((bf16[8,1,1,4,8192]{4,0,2,1,3:T(8,128)(2,1)}), bf16[8,1,1,4,8192]{4,0,2,1,3:T(8,128)(2,1)S(1)}, u32[]{:S(2)}, u32[]{:S(2)}) async-start(bf16[8,1,1,4,8192]{4,0,2,1,3:T(8,128)(2,1)} %copy.50), calls=%async_computation.1 | async-start | bytes 1048576 | tf_op jit(solution)/shard_map/all_to_all | solution.py:78
